TPU v7x, 128 devices: a whole 4x4x4 slice. The times are simulated.
128 devices in a mesh: req: 32 (over z_lo, y, x), tp: 4 (over z_hi, core).
Axes of the slice: x: 4, y: 4, z: 4 (z_hi: 2, z_lo: 2; z = z_hi * 2 + z_lo), core: 2. Of those that a mesh axis runs over, the one named last changes fastest.
Arguments:
- hidden_in: bfloat16 [8192, 2304], P('req'), may hold values from -6 to 6
- cache_lengths: int32 [32], P('req'), may hold values from 128 to 2048, as said below
- key_cache: bfloat16 [32, 2048, 2304], P('req', None, 'tp'), may hold values from -104 to 104
- value_cache: bfloat16 [32, 2048, 2304], P('req', None, 'tp'), may hold values from -6 to 6
- attn_norm: float32 [2304], replicated, may hold values from 0.5 to 1.5
- w_qkv: bfloat16 [3, 2304, 2304], P(None, None, 'tp'), may hold values from -0.125 to 0.125
- w_out: bfloat16 [2304, 2304], P('tp'), may hold values from -0.125 to 0.125
- ffn_norm: float32 [2304], replicated, may hold values from 0.5 to 1.5
- router: bfloat16 [2304, 8], replicated, may hold values from -0.125 to 0.125
- routes: int32 [8192, 2], P('req'), may hold values from 0 to 7, all different within a row; in each aligned block of 256 rows (0 to 255, 256 to 511, ...) at most 96 rows name the same one
- expert_gate: bfloat16 [32, 2304, 1440], P('req', None, 'tp'), may hold values from -0.125 to 0.125
- expert_up: bfloat16 [32, 2304, 1440], P('req', None, 'tp'), may hold values from -0.125 to 0.125
- expert_down: bfloat16 [32, 1440, 2304], P('req', 'tp'), may hold values from -0.078125 to 0.078125
Outputs:
- block_out: bfloat16 [8192, 2304], P(('req', 'tp'))
Inputs may be any that keep to these rules, and one draw needn't show every extreme that they name: `cache_lengths`: some request has exactly 2048 cached tokens. `routes`: within the 256 rows of one request no expert is named by more than 96 rows, and in every draw, within some request, an expert is named by exactly 96 rows; a row's two experts differ.
All inputs are finite; a program needn't handle non-finite values.
Results may differ from a plain program's by a relative error of at most 0.013.
Values may be sent and summed in bfloat16 or wider, within the bound.
A program may use at most 192 MiB of HBM per device.

v0:
```python
import math
import jax
import jax.numpy as jnp
from jax import lax
from jax.sharding import PartitionSpec as P

HEAD = 64
TOP = 2
CAP = 96
EPSILON = 1e-05


def normalize(inputs, scale_gain):
    mean_square = jnp.mean(inputs * inputs, axis=-1, keepdims=True)
    return inputs * lax.rsqrt(mean_square + EPSILON) * scale_gain


def rotate(inputs, positions):
    half_dim = inputs.shape[-1] // 2
    frequency = jnp.exp(
        jnp.arange(half_dim, dtype=jnp.float32) * (-2.0 * math.log(10000.0) / inputs.shape[-1])
    )
    angles = positions.astype(jnp.float32)[:, None] * frequency[None, :]
    cosine = jnp.cos(angles)[:, None, :]
    sine_part = jnp.sin(angles)[:, None, :]
    lower_half = inputs[..., :half_dim]
    upper_half = inputs[..., half_dim:]
    return jnp.concatenate(
        [
            lower_half * cosine - upper_half * sine_part,
            lower_half * sine_part + upper_half * cosine,
        ],
        axis=-1,
    )


def attention(queries, all_keys, all_values, length):
    query_count = queries.shape[0]
    cache_len = all_keys.shape[0] - query_count
    scores = jnp.einsum(
        "qhd,khd->hqk", queries, all_keys, preferred_element_type=jnp.float32
    ) * queries.shape[-1] ** (-0.5)
    slot_ids = jnp.arange(cache_len + query_count, dtype=jnp.int32)
    query_ids = jnp.arange(query_count, dtype=jnp.int32)
    is_live = jnp.where(
        slot_ids[None, :] < cache_len,
        slot_ids[None, :] < length,
        slot_ids[None, :] - cache_len <= query_ids[:, None],
    )
    scores = jnp.where(is_live[None], scores, -jnp.inf)
    row_max = jnp.max(scores, axis=-1, keepdims=True)
    weights = jnp.exp(scores - row_max)
    totals = jnp.sum(weights, axis=-1)
    mixture = jnp.einsum(
        "hqk,khd->qhd", weights.astype(jnp.bfloat16), all_values, preferred_element_type=jnp.float32
    )
    return (mixture / jnp.transpose(totals)[:, :, None]).astype(jnp.bfloat16)


def per_device(
    hidden_in,
    cache_lengths,
    key_cache,
    value_cache,
    attn_norm,
    w_qkv,
    w_out,
    ffn_norm,
    router,
    routes,
    expert_gate,
    expert_up,
    expert_down,
):
    token_count = hidden_in.shape[0]
    model_width = hidden_in.shape[1]
    local_lanes = w_qkv.shape[2]
    local_heads = local_lanes // HEAD
    cache_len = key_cache.shape[1]
    token_share = token_count // lax.axis_size("tp")
    offset = lax.axis_index("tp") * token_share
    expert_count = router.shape[1]
    copies = lax.axis_size("req") // expert_count
    residual = hidden_in.astype(jnp.float32)
    normed = normalize(residual, attn_norm).astype(jnp.bfloat16)
    projected = jnp.einsum("td,cdh->cth", normed, w_qkv, preferred_element_type=jnp.float32)
    length = cache_lengths[0]
    positions = length + jnp.arange(token_count, dtype=jnp.int32)
    queries = rotate(projected[0].reshape(token_count, local_heads, HEAD), positions).astype(
        jnp.bfloat16
    )
    fresh_keys = rotate(projected[1].reshape(token_count, local_heads, HEAD), positions).astype(
        jnp.bfloat16
    )
    fresh_values = projected[2].reshape(token_count, local_heads, HEAD).astype(jnp.bfloat16)
    all_keys = jnp.concatenate(
        [key_cache[0].reshape(cache_len, local_heads, HEAD), fresh_keys], axis=0
    )
    all_values = jnp.concatenate(
        [value_cache[0].reshape(cache_len, local_heads, HEAD), fresh_values], axis=0
    )
    attended = attention(queries, all_keys, all_values, length).reshape(token_count, local_lanes)
    summed_attn = lax.psum(
        jnp.dot(attended, w_out, preferred_element_type=jnp.float32).astype(jnp.bfloat16), "tp"
    ).astype(jnp.float32)
    updated = residual + summed_attn
    moe_input = normalize(updated, ffn_norm).astype(jnp.bfloat16)
    own_residual = lax.dynamic_slice_in_dim(updated, offset, token_share, 0)
    logits = jnp.dot(moe_input, router, preferred_element_type=jnp.float32)
    chosen = jnp.take_along_axis(logits, routes, axis=1)
    first_gate = 1.0 / (1.0 + jnp.exp(chosen[:, 1] - chosen[:, 0]))
    second_gate = 1.0 / (1.0 + jnp.exp(chosen[:, 0] - chosen[:, 1]))
    flat_routes = routes.reshape(-1)
    onehot = (flat_routes[:, None] == jnp.arange(expert_count, dtype=jnp.int32)[None, :]).astype(
        jnp.int32
    )
    slot_rank = jnp.sum((jnp.cumsum(onehot, axis=0) - onehot) * onehot, axis=1)
    tp_size = lax.axis_size("tp")
    core = lax.axis_index("tp") % 2
    half_cap = CAP // 2
    pairs = [(i, i ^ 1) for i in range(tp_size)]
    gate_w = jnp.concatenate([expert_gate[0], lax.ppermute(expert_gate[0], "tp", pairs)], axis=1)
    up_w = jnp.concatenate([expert_up[0], lax.ppermute(expert_up[0], "tp", pairs)], axis=1)
    down_w = jnp.concatenate([expert_down[0], lax.ppermute(expert_down[0], "tp", pairs)], axis=0)
    local_rank = slot_rank - core * half_cap
    in_half = (local_rank >= 0) & (local_rank < half_cap)
    slot_ids = jnp.where(in_half, flat_routes * half_cap + local_rank, -1)
    paired = slot_ids.reshape(token_count, TOP)
    slot_range = jnp.arange(expert_count * half_cap, dtype=jnp.int32)
    placing = jnp.any(paired[None, :, :] == slot_range[:, None, None], axis=2).astype(jnp.bfloat16)
    packed = (
        jnp.dot(placing, moe_input, preferred_element_type=jnp.float32)
        .astype(jnp.bfloat16)
        .reshape(expert_count, half_cap, model_width)
    )
    outgoing = jnp.broadcast_to(
        packed[:, None], (expert_count, copies, half_cap, model_width)
    ).reshape(expert_count * copies, half_cap, model_width)
    received = lax.all_to_all(outgoing, "req", split_axis=0, concat_axis=0, tiled=True)
    token_rows = received.reshape(-1, model_width)
    gate_proj = jnp.dot(token_rows, gate_w, preferred_element_type=jnp.float32)
    up_proj = jnp.dot(token_rows, up_w, preferred_element_type=jnp.float32)
    activation = (jax.nn.silu(gate_proj) * up_proj).astype(jnp.bfloat16)
    partial_value = jnp.dot(activation, down_w, preferred_element_type=jnp.float32).astype(
        jnp.bfloat16
    )
    returned = lax.all_to_all(
        partial_value.reshape(received.shape), "req", split_axis=0, concat_axis=0, tiled=True
    )
    summed = jnp.sum(
        returned.reshape(expert_count, copies, half_cap, model_width).astype(jnp.float32), axis=1
    ).reshape(expert_count * half_cap, model_width)
    gates = jnp.stack([first_gate, second_gate], axis=1)
    mixing = jnp.sum(
        jnp.where(paired[:, :, None] == slot_range[None, None, :], gates[:, :, None], 0.0), axis=1
    )
    local_sum = jnp.dot(mixing, summed, precision=lax.Precision.HIGHEST)
    moe_own = lax.psum_scatter(
        local_sum.astype(jnp.bfloat16), "tp", scatter_dimension=0, tiled=True
    ).astype(jnp.float32)
    return (own_residual + moe_own).astype(jnp.bfloat16)


def solution(mesh):
    return jax.shard_map(
        per_device,
        mesh=mesh,
        in_specs=(
            P("req", None),
            P("req"),
            P("req", None, "tp"),
            P("req", None, "tp"),
            P(),
            P(None, None, "tp"),
            P("tp", None),
            P(),
            P(),
            P("req", None),
            P("req", None, "tp"),
            P("req", None, "tp"),
            P("req", "tp", None),
        ),
        out_specs=P(("req", "tp"), None),
        check_vma=False,
    )
```

profile of v0, /device:TPU:1, one launch (start us, length us, event | category | flops | bytes accessed | tf_op | source)
XLA Modules:
  0.0 401.6 jit_solution(16575954713709232016)
XLA Ops:
  6.6 1.7 fusion.28
  8.3 6.0 %convolution_bitcast_fusion = f32[3,256,576]{1,2,0:T(8,128)S(1)} fusion(bf16[3,2304,576]{1,2,0:T(8,128)(2,1)} %param.18, bf16[256,2304]{1,0:T(8,128)(2,1)} %param.13, f32[2304]{0:T(1024)} %param.17, f32[256]{0:T(256)S(1)} %add_rsqrt_fusion.1), kind=kOutput, calls=%fused_computation.44 | convolution fusion | flops 2040791040 | bytes 10921984 | tf_op jit(solution)/shard_map/td,cdh->cth/dot_general | solution.py:86
  16.1 9.9 %fusion = (f32[9,256]{1,0:T(8,128)S(1)}, f32[9,256,2304]{2,1,0:T(8,128)}) fusion(pred[256,2304]{1,0:T(8,128)(4,1)S(1)} %fusion.31, bf16[256,9,32]{0,2,1:T(8,128)(2,1)S(1)} %get-tuple-element.13, bf16[256,9,32]{0,2,1:T(8,128)(2,1)S(1)} %get-tuple-element.14, bf16[2048,9,64]{0,2,1:T(8,128)(2,1)S(1)} %bitcast.62, ...), kind=kOutput, calls=%fused_computation.3 | convolution fusion | flops 703952640 | bytes 24781824 | tf_op jit(solution)/shard_map/qhd,khd->hqk/dot_general | solution.py:40
  26.0 10.6 %fusion.1 = f32[9,256]{1,0:T(8,128)S(1)} fusion(f32[9,256,2304]{2,1,0:T(8,128)} %get-tuple-element.20, f32[9,256]{1,0:T(8,128)S(1)} %get-tuple-element.19, pred[256,2304]{1,0:T(8,128)(4,1)S(1)} %fusion.31), kind=kLoop, calls=%fused_computation.4 | loop fusion | flops 21231360 | bytes 21841920 | tf_op jit(solution)/shard_map/reduce_sum | solution.py:53
  36.6 10.0 %fusion.48 = bf16[256,9,64]{0,2,1:T(8,128)(2,1)S(1)} fusion(f32[9,256,2304]{2,1,0:T(8,128)} %get-tuple-element.20, f32[9,256]{1,0:T(8,128)S(1)} %get-tuple-element.19, pred[256,2304]{1,0:T(8,128)(4,1)S(1)} %fusion.31, bf16[256,9,64]{0,2,1:T(8,128)(2,1)S(1)} %bitcast.60, bf16[2048,9,64]{0,2,1:T(8,128)(2,1)S(1)} %bitcast.63, f32[256,9]{0,1:T(8,128)S(1)} %bitcast.61), kind=kOutput, calls=%fused_computation.50 | convolution fusion | flops 706314240 | bytes 24791040 | tf_op jit(solution)/shard_map/hqk,khd->qhd/dot_general | solution.py:54
  46.7 2.2 convolution_convert_fusion.3
  49.3 1.1 reduce-window.6
  51.2 48.0 %all-reduce.2.cloned.1.call-done = bf16[256,2304]{1,0:T(8,128)(2,1)} async-done(((bf16[256,2304]{1,0:T(8,128)(2,1)}), bf16[256,2304]{1,0:T(8,128)(2,1)}) %all-reduce.2.cloned.1.call-update) | async-done | bytes 1179664 | tf_op jit(solution)/shard_map/psum | solution.py:103
  99.3 3.1 convert_add_fusion
  102.4 0.8 convolution_convert_fusion.1
  103.2 3.5 broadcast_in_dim.87
  106.7 7.0 %all-to-all-start = ((bf16[32,48,2304]{2,1,0:T(8,128)(2,1)}), bf16[32,48,2304]{2,1,0:T(8,128)(2,1)}, u32[]{:S(2)}, u32[]{:S(2)}) async-start(bf16[32,48,2304]{2,1,0:T(8,128)(2,1)} %bitcast.53), calls=%async_computation | async-start | bytes 14155776 | tf_op jit(solution)/shard_map/all_to_all | solution.py:139
  113.7 0.5 collective-permute-start
  114.7 3.0 collective-permute-done
  117.7 97.1 %all-to-all-done = bf16[32,48,2304]{2,1,0:T(8,128)(2,1)} async-done(((bf16[32,48,2304]{2,1,0:T(8,128)(2,1)}), bf16[32,48,2304]{2,1,0:T(8,128)(2,1)}, u32[]{:S(2)}, u32[]{:S(2)}) %all-to-all-start) | async-done | bytes 7077920 | tf_op jit(solution)/shard_map/all_to_all | solution.py:139
  214.9 9.9 %fusion.6 = f32[1536,720]{0,1:T(8,128)} fusion(bf16[1536,2304]{1,0:T(8,128)(2,1)} %bitcast.16, bf16[2304,360]{0,1:T(8,128)(2,1)} %collective-permute-done, bf16[2304,360]{0,1:T(8,128)(2,1)} %bitcast.65), kind=kOutput, calls=%fused_computation.17 | convolution fusion | flops 5102714880 | bytes 14819328 | tf_op jit(solution)/shard_map/dot_general | solution.py:141
  224.8 21.1 %convolution_convert_fusion = bf16[1536,2304]{1,0:T(8,128)(2,1)} fusion(bf16[360,2304]{1,0:T(8,128)(2,1)} %collective-permute-done.2, bf16[360,2304]{1,0:T(8,128)(2,1)} %bitcast.67, f32[1536,720]{0,1:T(8,128)} %fusion.6, bf16[1536,2304]{1,0:T(8,128)(2,1)} %bitcast.16, bf16[2304,360]{0,1:T(8,128)(2,1)} %collective-permute-done.1, bf16[2304,360]{0,1:T(8,128)(2,1)} %bitcast.69), kind=kOutput, calls=%fused_computation.7 | convolution fusion | flops 10215604224 | bytes 25214976 | tf_op jit(solution)/shard_map/dot_general | solution.py:144
  245.9 8.8 %all-to-all-start.1 = ((bf16[32,48,2304]{2,1,0:T(8,128)(2,1)}), bf16[32,48,2304]{2,1,0:T(8,128)(2,1)}, u32[]{:S(2)}, u32[]{:S(2)}) async-start(bf16[32,48,2304]{2,1,0:T(8,128)(2,1)} %bitcast.55), calls=%async_computation.1 | async-start | bytes 14155776 | tf_op jit(solution)/shard_map/all_to_all | solution.py:147
  255.6 3.7 gather_fusion
  259.8 87.7 %all-to-all-done.1 = bf16[32,48,2304]{2,1,0:T(8,128)(2,1)} async-done(((bf16[32,48,2304]{2,1,0:T(8,128)(2,1)}), bf16[32,48,2304]{2,1,0:T(8,128)(2,1)}, u32[]{:S(2)}, u32[]{:S(2)}) %all-to-all-start.1) | async-done | bytes 7077920 | tf_op jit(solution)/shard_map/all_to_all | solution.py:147
  347.5 4.4 %convert_reduce_fusion = f32[8,48,2304]{2,1,0:T(8,128)S(1)} fusion(bf16[32,48,2304]{2,1,0:T(8,128)(2,1)} %all-to-all-done.1), kind=kLoop, calls=%fused_computation.6 | loop fusion | flops 6193152 | bytes 10616832 | tf_op jit(solution)/shard_map/reduce_sum | solution.py:150
  351.9 5.0 %convolution_convert_fusion.2 = bf16[256,2304]{1,0:T(8,128)(2,1)} fusion(f32[256,384]{1,0:T(8,128)S(1)} %select_reduce_fusion, f32[384,2304]{1,0:T(8,128)S(1)} %bitcast.54), kind=kOutput, calls=%fused_computation.12 | convolution fusion | flops 2718498816 | bytes 5111808 | tf_op jit(solution)/shard_map/dot_general | solution.py:157
  357.0 35.9 %reduce-scatter.2.cloned.1.call-done = bf16[64,2304]{1,0:T(8,128)(2,1)} async-done(((bf16[256,2304]{1,0:T(8,128)(2,1)}), bf16[64,2304]{1,0:T(8,128)(2,1)}) %reduce-scatter.2.cloned.1.call-update) | async-done | bytes 294928 | tf_op jit(solution)/shard_map/reduce_scatter | solution.py:158
  392.9 1.9 add_convert_fusion
  (60 shorter events, 4.0 us)
Async XLA Ops:
  6.5 40.1 %copy-start = (bf16[576,2304]{1,0:T(8,128)(2,1)S(1)}, bf16[576,2304]{1,0:T(8,128)(2,1)}, u32[]{:S(2)}) copy-start(bf16[576,2304]{1,0:T(8,128)(2,1)} %param.19) | copy-start | bytes 7962628
  6.5 92.7 %all-reduce.2.cloned.1.call-start = ((), (), s32[]{:S(2)}) async-start(), calls=%async_computation.3 | async-start | bytes 2359296 | tf_op jit(solution)/shard_map/psum | solution.py:103
  14.3 1.7 copy-start.5
  26.0 10.6 %copy-start.6 = (bf16[1,2048,576]{1,2,0:T(8,128)(2,1)S(1)}, bf16[1,2048,576]{1,2,0:T(8,128)(2,1)}, u32[]{:S(2)}) copy-start(bf16[1,2048,576]{1,2,0:T(8,128)(2,1)} %param.16) | copy-start | bytes 7077892
  46.7 2.2 copy-start.4
  48.8 50.4 %copy-start.2 = (bf16[256,2304]{1,0:T(8,128)(2,1)S(1)}, bf16[256,2304]{1,0:T(8,128)(2,1)}, u32[]{:S(2)}) copy-start(bf16[256,2304]{1,0:T(8,128)(2,1)} %param.13) | copy-start | bytes 3538948
  49.2 53.2 %copy-start.8 = (f32[2304]{0:T(1024)S(1)}, f32[2304]{0:T(1024)}, u32[]{:S(2)}) copy-start(f32[2304]{0:T(1024)} %param.20) | copy-start | bytes 27652
  99.3 3.1 copy-start.3
  106.7 108.2 %all-to-all-start = ((bf16[32,48,2304]{2,1,0:T(8,128)(2,1)}), bf16[32,48,2304]{2,1,0:T(8,128)(2,1)}, u32[]{:S(2)}, u32[]{:S(2)}) async-start(bf16[32,48,2304]{2,1,0:T(8,128)(2,1)} %bitcast.53), calls=%async_computation | async-start | bytes 14155776 | tf_op jit(solution)/shard_map/all_to_all | solution.py:139
  113.7 4.0 %collective-permute-start = (bf16[2304,360]{0,1:T(8,128)(2,1)}, bf16[2304,360]{0,1:T(8,128)(2,1)}, u32[]{:S(2)}, u32[]{:S(2)}) collective-permute-start(bf16[2304,360]{0,1:T(8,128)(2,1)} %bitcast.64), channel_id=1, source_target_pairs={{0,1},{1,0},{2,3},{3,2},{4,5},{5,4},{6,7},{7,6},{8,9},{9,8},{10,11... | collective-permute-start | bytes 4976648 | tf_op jit(solution)/shard_map/ppermute | solution.py:122
  114.2 110.6 %collective-permute-start.2 = (bf16[360,2304]{1,0:T(8,128)(2,1)}, bf16[360,2304]{1,0:T(8,128)(2,1)}, u32[]{:S(2)}, u32[]{:S(2)}) collective-permute-start(bf16[360,2304]{1,0:T(8,128)(2,1)} %bitcast.66), channel_id=1, source_target_pairs={{0,1},{1,0},{2,3},{3,2},{4,5},{5,4},{6,7},{7,6},{8,9},{9,8},{10,11... | collective-permute-start | bytes 4976648 | tf_op jit(solution)/shard_map/ppermute | solution.py:124
  114.3 110.5 %collective-permute-start.1 = (bf16[2304,360]{0,1:T(8,128)(2,1)}, bf16[2304,360]{0,1:T(8,128)(2,1)}, u32[]{:S(2)}, u32[]{:S(2)}) collective-permute-start(bf16[2304,360]{0,1:T(8,128)(2,1)} %bitcast.68), channel_id=1, source_target_pairs={{0,1},{1,0},{2,3},{3,2},{4,5},{5,4},{6,7},{7,6},{8,9},{9,8},{10,11... | collective-permute-start | bytes 4976648 | tf_op jit(solution)/shard_map/ppermute | solution.py:123
  245.9 9.1 %copy-start.7 = (bf16[2304,8]{0,1:T(8,128)(2,1)S(1)}, bf16[2304,8]{0,1:T(8,128)(2,1)}, u32[]{:S(2)}) copy-start(bf16[2304,8]{0,1:T(8,128)(2,1)} %param.21) | copy-start | bytes 110596
  245.9 101.6 %all-to-all-start.1 = ((bf16[32,48,2304]{2,1,0:T(8,128)(2,1)}), bf16[32,48,2304]{2,1,0:T(8,128)(2,1)}, u32[]{:S(2)}, u32[]{:S(2)}) async-start(bf16[32,48,2304]{2,1,0:T(8,128)(2,1)} %bitcast.55), calls=%async_computation.1 | async-start | bytes 14155776 | tf_op jit(solution)/shard_map/all_to_all | solution.py:147
  254.7 138.1 %reduce-scatter.2.cloned.1.call-start = ((), (), s32[]{:S(2)}) async-start(), calls=%async_computation.4 | async-start | bytes 1474560 | tf_op jit(solution)/shard_map/reduce_scatter | solution.py:158
  351.9 42.8 %copy-start.1 = (bf16[576,2304]{1,0:T(8,128)(2,1)S(1)}, bf16[576,2304]{1,0:T(8,128)(2,1)}, u32[]{:S(2)}) copy-start(bf16[576,2304]{1,0:T(8,128)(2,1)} %param.19) | copy-start | bytes 7962628
Sparse Core Ops, SparseCore 0:
  49.0 50.2 all-reduce.1
  357.1 35.7 reduce-scatter.1
where the time goes:
time: 402 us
  waiting for transfers between devices  272 us (68%)
  matrix products  65.5 us (16%)
  other arithmetic  24.3 us (6%)
  starting transfers between devices  16.9 us (4%)
  between operations  14.5 us (4%)
  local copies, waits for them, and re-layouts  8.63 us (2%)
    all_to_all x1, waiting for transfers between devices, per_device(): lax.all_to_all(outgoing, 'req', split_axis=0, concat_axis=0, tiled=True)  97.1 us
    all_to_all x1, waiting for transfers between devices, per_device(): lax.all_to_all(partial_value.reshape(received.shape), 'req', split_axis=0...  87.7 us
    psum x1, waiting for transfers between devices, per_device(): lax.psum(jnp.dot(attended, w_out, preferred_element_type=jnp.float32).ast...  48 us
    reduce_scatter x1, waiting for transfers between devices, per_device(): lax.psum_scatter(local_sum.astype(jnp.bfloat16), 'tp', scatter_dimension=...  35.9 us
    dot_general x1, matrix products, per_device(): jnp.dot(activation, down_w, preferred_element_type=jnp.float32)  21.1 us
    reduce_sum x1, other arithmetic, attention(): totals = jnp.sum(weights, axis=-1)  10.6 us
    dot_general x1, matrix products, attention(): jnp.einsum('hqk,khd->qhd', weights.astype(jnp.bfloat16), all_values, pref...  10 us
    dot_general x1, matrix products, per_device(): gate_proj = jnp.dot(token_rows, gate_w, preferred_element_type=jnp.float32)  9.94 us
  transfers between devices with their start and end apart: 7, of which 5 were waited for; matrix products, arithmetic and copies ran while one was open for 4% of the time, Pallas kernels for 0%

commit v1 on v0

--- a/solution.py
+++ b/solution.py
@@ -100,8 +100,11 @@
         [value_cache[0].reshape(cache_len, local_heads, HEAD), fresh_values], axis=0
     )
     attended = attention(queries, all_keys, all_values, length).reshape(token_count, local_lanes)
-    summed_attn = lax.psum(
-        jnp.dot(attended, w_out, preferred_element_type=jnp.float32).astype(jnp.bfloat16), "tp"
+    summed_attn = jnp.sum(
+        lax.all_gather(
+            jnp.dot(attended, w_out, preferred_element_type=jnp.float32).astype(jnp.bfloat16), "tp"
+        ),
+        axis=0,
     ).astype(jnp.float32)
     updated = residual + summed_attn
     moe_input = normalize(updated, ffn_norm).astype(jnp.bfloat16)

time: 402 us -> 399 us (level)
  waiting for transfers between devices: 272 us -> 265 us
    psum x1 -> x0, waiting for transfers between devices: 48 us -> none  [per_device(): lax.psum(jnp.dot(attended, w_out, preferred_element_type=jnp.float32).ast...]
    all_gather x0 -> x1, waiting for transfers between devices: none -> 43.1 us  [per_device(): lax.all_gather(jnp.dot(attended, w_out, preferred_element_type=jnp.float3...]
where the time goes in v1:
time: 399 us; the launch traced here: 398 us
  waiting for transfers between devices  265 us (66%)
  matrix products  65.5 us (16%)
  other arithmetic  26.7 us (7%)
  starting transfers between devices  17.6 us (4%)
  between operations  14.5 us (4%)
  local copies, waits for them, and re-layouts  8.48 us (2%)
    all_to_all x1, waiting for transfers between devices, per_device(): lax.all_to_all(outgoing, 'req', split_axis=0, concat_axis=0, tiled=True)  96.7 us
    all_to_all x1, waiting for transfers between devices, per_device(): lax.all_to_all(partial_value.reshape(received.shape), 'req', split_axis=0...  88 us
    all_gather x1, waiting for transfers between devices, per_device(): lax.all_gather(jnp.dot(attended, w_out, preferred_element_type=jnp.float3...  43.1 us
    reduce_scatter x1, waiting for transfers between devices, per_device(): lax.psum_scatter(local_sum.astype(jnp.bfloat16), 'tp', scatter_dimension=...  34.7 us
    dot_general x1, matrix products, per_device(): jnp.dot(activation, down_w, preferred_element_type=jnp.float32)  21.1 us
    reduce_sum x1, other arithmetic, attention(): totals = jnp.sum(weights, axis=-1)  10.6 us
    dot_general x1, matrix products, attention(): jnp.einsum('hqk,khd->qhd', weights.astype(jnp.bfloat16), all_values, pref...  10 us
    dot_general x1, matrix products, per_device(): gate_proj = jnp.dot(token_rows, gate_w, preferred_element_type=jnp.float32)  9.94 us
  transfers between devices with their start and end apart: 7, of which 5 were waited for; matrix products, arithmetic and copies ran while one was open for 4% of the time, Pallas kernels for 0%

profile of v1, /device:TPU:1, one launch (start us, length us, event | category | flops | bytes accessed | tf_op | source)
XLA Modules:
  0.0 398.3 jit_solution(15450293821210532642)
XLA Ops:
  6.6 1.7 fusion.28
  8.3 6.0 %convolution_bitcast_fusion = f32[3,256,576]{1,2,0:T(8,128)S(1)} fusion(bf16[3,2304,576]{1,2,0:T(8,128)(2,1)} %param.18, bf16[256,2304]{1,0:T(8,128)(2,1)} %param.13, f32[2304]{0:T(1024)} %param.17, f32[256]{0:T(256)S(1)} %add_rsqrt_fusion.1), kind=kOutput, calls=%fused_computation.44 | convolution fusion | flops 2040791040 | bytes 10921984 | tf_op jit(solution)/shard_map/td,cdh->cth/dot_general | solution.py:86
  16.1 9.9 %fusion = (f32[9,256]{1,0:T(8,128)S(1)}, f32[9,256,2304]{2,1,0:T(8,128)}) fusion(pred[256,2304]{1,0:T(8,128)(4,1)S(1)} %fusion.31, bf16[256,9,32]{0,2,1:T(8,128)(2,1)S(1)} %get-tuple-element.13, bf16[256,9,32]{0,2,1:T(8,128)(2,1)S(1)} %get-tuple-element.14, bf16[2048,9,64]{0,2,1:T(8,128)(2,1)S(1)} %bitcast.64, ...), kind=kOutput, calls=%fused_computation.3 | convolution fusion | flops 703952640 | bytes 24781824 | tf_op jit(solution)/shard_map/qhd,khd->hqk/dot_general | solution.py:40
  26.0 10.6 %fusion.1 = f32[9,256]{1,0:T(8,128)S(1)} fusion(f32[9,256,2304]{2,1,0:T(8,128)} %get-tuple-element.20, f32[9,256]{1,0:T(8,128)S(1)} %get-tuple-element.19, pred[256,2304]{1,0:T(8,128)(4,1)S(1)} %fusion.31), kind=kLoop, calls=%fused_computation.4 | loop fusion | flops 21231360 | bytes 21841920 | tf_op jit(solution)/shard_map/reduce_sum | solution.py:53
  36.6 10.0 %fusion.48 = bf16[256,9,64]{0,2,1:T(8,128)(2,1)S(1)} fusion(f32[9,256,2304]{2,1,0:T(8,128)} %get-tuple-element.20, f32[9,256]{1,0:T(8,128)S(1)} %get-tuple-element.19, pred[256,2304]{1,0:T(8,128)(4,1)S(1)} %fusion.31, bf16[256,9,64]{0,2,1:T(8,128)(2,1)S(1)} %bitcast.62, bf16[2048,9,64]{0,2,1:T(8,128)(2,1)S(1)} %bitcast.65, f32[256,9]{0,1:T(8,128)S(1)} %bitcast.63), kind=kOutput, calls=%fused_computation.50 | convolution fusion | flops 706314240 | bytes 24791040 | tf_op jit(solution)/shard_map/hqk,khd->qhd/dot_general | solution.py:54
  46.7 2.2 convolution_convert_fusion.3
  49.3 1.1 reduce-window.6
  51.2 43.1 %all-gather.3.cloned.1.call-done = bf16[1024,2304]{1,0:T(8,128)(2,1)} async-done(((bf16[256,2304]{1,0:T(8,128)(2,1)}), bf16[1024,2304]{1,0:T(8,128)(2,1)}) %all-gather.3.cloned.1.call-update) | async-done | bytes 4718608 | tf_op jit(solution)/shard_map/all_gather | solution.py:104
  94.3 3.8 reduce_sum.68
  98.1 1.8 convert_add_fusion
  99.9 0.8 convolution_convert_fusion.1
  100.7 3.5 broadcast_in_dim.87
  104.1 7.0 %all-to-all-start = ((bf16[32,48,2304]{2,1,0:T(8,128)(2,1)}), bf16[32,48,2304]{2,1,0:T(8,128)(2,1)}, u32[]{:S(2)}, u32[]{:S(2)}) async-start(bf16[32,48,2304]{2,1,0:T(8,128)(2,1)} %bitcast.54), calls=%async_computation | async-start | bytes 14155776 | tf_op jit(solution)/shard_map/all_to_all | solution.py:142
  112.3 3.0 collective-permute-done
  115.3 96.7 %all-to-all-done = bf16[32,48,2304]{2,1,0:T(8,128)(2,1)} async-done(((bf16[32,48,2304]{2,1,0:T(8,128)(2,1)}), bf16[32,48,2304]{2,1,0:T(8,128)(2,1)}, u32[]{:S(2)}, u32[]{:S(2)}) %all-to-all-start) | async-done | bytes 7077920 | tf_op jit(solution)/shard_map/all_to_all | solution.py:142
  211.9 9.9 %fusion.6 = f32[1536,720]{0,1:T(8,128)} fusion(bf16[1536,2304]{1,0:T(8,128)(2,1)} %bitcast.17, bf16[2304,360]{0,1:T(8,128)(2,1)} %collective-permute-done, bf16[2304,360]{0,1:T(8,128)(2,1)} %bitcast.67), kind=kOutput, calls=%fused_computation.17 | convolution fusion | flops 5102714880 | bytes 14819328 | tf_op jit(solution)/shard_map/dot_general | solution.py:144
  221.9 21.1 %convolution_convert_fusion = bf16[1536,2304]{1,0:T(8,128)(2,1)} fusion(bf16[360,2304]{1,0:T(8,128)(2,1)} %collective-permute-done.2, bf16[360,2304]{1,0:T(8,128)(2,1)} %bitcast.69, f32[1536,720]{0,1:T(8,128)} %fusion.6, bf16[1536,2304]{1,0:T(8,128)(2,1)} %bitcast.17, bf16[2304,360]{0,1:T(8,128)(2,1)} %collective-permute-done.1, bf16[2304,360]{0,1:T(8,128)(2,1)} %bitcast.71), kind=kOutput, calls=%fused_computation.7 | convolution fusion | flops 10215604224 | bytes 25214976 | tf_op jit(solution)/shard_map/dot_general | solution.py:147
  243.0 9.1 %all-to-all-start.1 = ((bf16[32,48,2304]{2,1,0:T(8,128)(2,1)}), bf16[32,48,2304]{2,1,0:T(8,128)(2,1)}, u32[]{:S(2)}, u32[]{:S(2)}) async-start(bf16[32,48,2304]{2,1,0:T(8,128)(2,1)} %bitcast.56), calls=%async_computation.1 | async-start | bytes 14155776 | tf_op jit(solution)/shard_map/all_to_all | solution.py:150
  253.3 3.5 gather_fusion
  257.4 88.0 %all-to-all-done.1 = bf16[32,48,2304]{2,1,0:T(8,128)(2,1)} async-done(((bf16[32,48,2304]{2,1,0:T(8,128)(2,1)}), bf16[32,48,2304]{2,1,0:T(8,128)(2,1)}, u32[]{:S(2)}, u32[]{:S(2)}) %all-to-all-start.1) | async-done | bytes 7077920 | tf_op jit(solution)/shard_map/all_to_all | solution.py:150
  345.3 4.4 %convert_reduce_fusion = f32[8,48,2304]{2,1,0:T(8,128)S(1)} fusion(bf16[32,48,2304]{2,1,0:T(8,128)(2,1)} %all-to-all-done.1), kind=kLoop, calls=%fused_computation.6 | loop fusion | flops 6193152 | bytes 10616832 | tf_op jit(solution)/shard_map/reduce_sum | solution.py:153
  349.8 5.0 %convolution_convert_fusion.2 = bf16[256,2304]{1,0:T(8,128)(2,1)} fusion(f32[256,384]{1,0:T(8,128)S(1)} %select_reduce_fusion, f32[384,2304]{1,0:T(8,128)S(1)} %bitcast.55), kind=kOutput, calls=%fused_computation.12 | convolution fusion | flops 2718498816 | bytes 5111808 | tf_op jit(solution)/shard_map/dot_general | solution.py:160
  354.8 34.7 %reduce-scatter.2.cloned.1.call-done = bf16[64,2304]{1,0:T(8,128)(2,1)} async-done(((bf16[256,2304]{1,0:T(8,128)(2,1)}), bf16[64,2304]{1,0:T(8,128)(2,1)}) %reduce-scatter.2.cloned.1.call-update) | async-done | bytes 294928 | tf_op jit(solution)/shard_map/reduce_scatter | solution.py:161
  389.5 1.9 add_convert_fusion
  (59 shorter events, 4.9 us)
Async XLA Ops:
  6.5 40.1 %copy-start = (bf16[576,2304]{1,0:T(8,128)(2,1)S(1)}, bf16[576,2304]{1,0:T(8,128)(2,1)}, u32[]{:S(2)}) copy-start(bf16[576,2304]{1,0:T(8,128)(2,1)} %param.19) | copy-start | bytes 7962628
  6.5 87.8 %all-gather.3.cloned.1.call-start = ((), (), s32[]{:S(2)}) async-start(), calls=%async_computation.4 | async-start | bytes 5898240 | tf_op jit(solution)/shard_map/all_gather | solution.py:104
  14.3 1.7 copy-start.4
  26.0 10.6 %copy-start.5 = (bf16[1,2048,576]{1,2,0:T(8,128)(2,1)S(1)}, bf16[1,2048,576]{1,2,0:T(8,128)(2,1)}, u32[]{:S(2)}) copy-start(bf16[1,2048,576]{1,2,0:T(8,128)(2,1)} %param.16) | copy-start | bytes 7077892
  46.7 2.2 copy-start.3
  94.3 3.8 copy-start.2
  98.1 1.8 copy-start.7
  104.1 107.8 %all-to-all-start = ((bf16[32,48,2304]{2,1,0:T(8,128)(2,1)}), bf16[32,48,2304]{2,1,0:T(8,128)(2,1)}, u32[]{:S(2)}, u32[]{:S(2)}) async-start(bf16[32,48,2304]{2,1,0:T(8,128)(2,1)} %bitcast.54), calls=%async_computation | async-start | bytes 14155776 | tf_op jit(solution)/shard_map/all_to_all | solution.py:142
  111.2 4.1 %collective-permute-start = (bf16[2304,360]{0,1:T(8,128)(2,1)}, bf16[2304,360]{0,1:T(8,128)(2,1)}, u32[]{:S(2)}, u32[]{:S(2)}) collective-permute-start(bf16[2304,360]{0,1:T(8,128)(2,1)} %bitcast.66), channel_id=1, source_target_pairs={{0,1},{1,0},{2,3},{3,2},{4,5},{5,4},{6,7},{7,6},{8,9},{9,8},{10,11... | collective-permute-start | bytes 4976648 | tf_op jit(solution)/shard_map/ppermute | solution.py:125
  111.8 110.1 %collective-permute-start.2 = (bf16[360,2304]{1,0:T(8,128)(2,1)}, bf16[360,2304]{1,0:T(8,128)(2,1)}, u32[]{:S(2)}, u32[]{:S(2)}) collective-permute-start(bf16[360,2304]{1,0:T(8,128)(2,1)} %bitcast.68), channel_id=1, source_target_pairs={{0,1},{1,0},{2,3},{3,2},{4,5},{5,4},{6,7},{7,6},{8,9},{9,8},{10,11... | collective-permute-start | bytes 4976648 | tf_op jit(solution)/shard_map/ppermute | solution.py:127
  112.1 109.8 %collective-permute-start.1 = (bf16[2304,360]{0,1:T(8,128)(2,1)}, bf16[2304,360]{0,1:T(8,128)(2,1)}, u32[]{:S(2)}, u32[]{:S(2)}) collective-permute-start(bf16[2304,360]{0,1:T(8,128)(2,1)} %bitcast.70), channel_id=1, source_target_pairs={{0,1},{1,0},{2,3},{3,2},{4,5},{5,4},{6,7},{7,6},{8,9},{9,8},{10,11... | collective-permute-start | bytes 4976648 | tf_op jit(solution)/shard_map/ppermute | solution.py:126
  243.0 9.8 %copy-start.6 = (bf16[2304,8]{0,1:T(8,128)(2,1)S(1)}, bf16[2304,8]{0,1:T(8,128)(2,1)}, u32[]{:S(2)}) copy-start(bf16[2304,8]{0,1:T(8,128)(2,1)} %param.21) | copy-start | bytes 110596
  243.0 102.3 %all-to-all-start.1 = ((bf16[32,48,2304]{2,1,0:T(8,128)(2,1)}), bf16[32,48,2304]{2,1,0:T(8,128)(2,1)}, u32[]{:S(2)}, u32[]{:S(2)}) async-start(bf16[32,48,2304]{2,1,0:T(8,128)(2,1)} %bitcast.56), calls=%async_computation.1 | async-start | bytes 14155776 | tf_op jit(solution)/shard_map/all_to_all | solution.py:150
  252.2 137.3 %reduce-scatter.2.cloned.1.call-start = ((), (), s32[]{:S(2)}) async-start(), calls=%async_computation.3 | async-start | bytes 1474560 | tf_op jit(solution)/shard_map/reduce_scatter | solution.py:161
  349.7 41.7 %copy-start.1 = (bf16[576,2304]{1,0:T(8,128)(2,1)S(1)}, bf16[576,2304]{1,0:T(8,128)(2,1)}, u32[]{:S(2)}) copy-start(bf16[576,2304]{1,0:T(8,128)(2,1)} %param.19) | copy-start | bytes 7962628
Sparse Core Ops, SparseCore 0:
  49.0 45.2 all-gather.2
  354.9 34.5 reduce-scatter.1
